TPU v7x, 32 devices: a whole 2x2x4 slice. The times are simulated.
32 devices in a mesh: seq: 8 (over y, x, core), tensor: 4 (over z).
Axes of the slice: x: 2, y: 2, z: 4, core: 2. Of those that a mesh axis runs over, the one named last changes fastest.
Arguments:
- queries: bfloat16 [1024, 4096], P(('seq', 'tensor')), may hold values from -5 to 5
- keys: bfloat16 [1024, 1024], P(('seq', 'tensor')), may hold values from -5 to 5
- values: bfloat16 [1024, 1024], P(('seq', 'tensor')), may hold values from -5 to 5
- mamba_x: bfloat16 [1024, 8192], P(('seq', 'tensor')), may hold values from -5 to 5
- mamba_b: bfloat16 [1024, 1024], P(('seq', 'tensor')), may hold values from -5 to 5
- mamba_c: bfloat16 [1024, 1024], P(('seq', 'tensor')), may hold values from -5 to 5
- mamba_dt: bfloat16 [1024, 128], P(('seq', 'tensor')), may hold values from -4 to 4
- conv_x: bfloat16 [4, 8192], P(None, 'tensor'), may hold values from -3 to 3
- conv_b: bfloat16 [4, 1024], P(None, 'tensor'), may hold values from -3 to 3
- conv_c: bfloat16 [4, 1024], P(None, 'tensor'), may hold values from -3 to 3
- dt_bias: float32 [128], P('tensor'), may hold values from -1 to 1
- decay_rate: float32 [128], P('tensor'), may hold values from 0.0001 to 0.05
- skip_gain: float32 [128], P('tensor'), may hold values from 0.5 to 1.5
- norm_gain: float32 [8192], P('tensor'), may hold values from 0.5 to 1.5
- windows: int32 [32], replicated, may hold values from 160 to 640, as said below
- doc_lengths: int32 [3], replicated, may hold values from 1 to 768, 1024 in all
Outputs:
- attn_out: bfloat16 [1024, 4096], P('seq', 'tensor')
- mamba_out: bfloat16 [1024, 8192], P('seq', 'tensor')
- attn_checksum: float32 [4096], P('tensor')
- mamba_checksum: float32 [8192], P('tensor')
Inputs may be any that keep to these rules, and one draw needn't show every extreme that they name: `windows`: one of the 32 query heads has a window of exactly 640 tokens. `doc_lengths`: 3 lengths summing to 1024; the longest is exactly three quarters of 1024.
All inputs are finite; a program needn't handle non-finite values.
Results may differ from a plain program's by a relative error of at most 0.007.
Values may be sent and summed in bfloat16 or wider, within the bound.
No kernel may reach another device: no remote copies, remote signals or barrier semaphores. Data moves between devices by JAX's collectives and lax.ppermute only.
A program may use at most 192 MiB of HBM per device.

v0:
```python
import math
import jax
import jax.numpy as jnp
from jax import lax
from jax.sharding import PartitionSpec as P

HEAD_SIZE = 128
MP = 64
MN = 128
KC = 4
NEG_LARGE = -1e30
EPS_NORM = 1e-05


def shifted(block, axis, distance):
    devices = range(lax.axis_size(axis))
    route = [(i - distance, i) for i in devices if i - distance in devices]
    return lax.ppermute(block, axis, route)


def prefix(x, axis, combine, identity):
    length, here = (lax.axis_size(axis), lax.axis_index(axis))
    everything = jax.tree.map(
        lambda part, kind: lax.all_gather(part.astype(kind), axis), x, (jnp.bfloat16, jnp.bfloat16)
    )
    start = jax.tree.map(
        lambda part, zero: jnp.broadcast_to(jnp.asarray(zero, part.dtype), part.shape), x, identity
    )

    def turn(k, before):
        reached = k < here
        new = combine(
            before, jax.tree.map(lambda part, own: part[k].astype(own.dtype), everything, x)
        )
        return jax.tree.map(lambda a, b: jnp.where(reached, a, b), new, before)

    return lax.fori_loop(0, length, turn, start)


def doc_table(doc_lengths):
    return jnp.cumsum(doc_lengths) - doc_lengths


def doc_index(positions, doc_starts):
    return jnp.sum((positions[:, None] >= doc_starts[None, :]).astype(jnp.int32), axis=1) - 1


def allowed_mask(query_pos, key_pos, doc_starts, window_per_head):
    gap = query_pos[:, None] - key_pos[None, :]
    same_doc = doc_index(query_pos, doc_starts)[:, None] == doc_index(key_pos, doc_starts)[None, :]
    base_ok = (gap >= 0) & (key_pos[None, :] >= 0) & same_doc
    return base_ok[None, None] & (gap[None, None] < window_per_head[:, :, None, None])


def attend_piece(
    carry, piece, key_start, grouped_heads, query_pos, doc_starts, window_per_head, reach
):
    key_rows, value_rows = piece
    key_count = key_rows.shape[0]
    shared_heads = grouped_heads.shape[1]
    key_pos = jnp.arange(key_count, dtype=jnp.int32)

    def compute(state):
        old_max, old_total, old_accum = state
        keys_rank3 = key_rows.reshape(key_count, shared_heads, HEAD_SIZE)
        values_rank3 = value_rows.reshape(key_count, shared_heads, HEAD_SIZE)
        scores = jnp.einsum(
            "tgqd,sgd->gqts", grouped_heads, keys_rank3, preferred_element_type=jnp.float32
        ) * (1.0 / math.sqrt(HEAD_SIZE))
        allowed = allowed_mask(query_pos, key_pos, doc_starts, window_per_head)
        scores = jnp.where(allowed, scores, NEG_LARGE)
        new_max = jnp.maximum(old_max, jnp.max(scores, axis=-1))
        weights = jnp.where(allowed, jnp.exp(scores - new_max[..., None]), 0.0)
        new_total = jnp.sum(weights, axis=-1)
        product = jnp.einsum(
            "gqts,sgd->gqtd",
            weights.astype(jnp.bfloat16),
            values_rank3,
            preferred_element_type=jnp.float32,
        )
        return (new_max, new_total, product)

    touches = (key_start + key_count - 1 >= query_pos[0] - reach) & (key_start <= query_pos[-1])
    return lax.cond(touches, compute, lambda state: state, carry)


def causal_conv(extended, taps, positions, doc_starts):
    count = positions.shape[0]
    docs_out = doc_index(positions, doc_starts)
    ext_pos = positions[0] - (KC - 1) + jnp.arange(count + KC - 1, dtype=jnp.int32)
    docs_ext = doc_index(ext_pos, doc_starts)
    running = jnp.zeros((count, extended.shape[1]), jnp.float32)
    for tap_index in range(KC):
        offset = KC - 1 - tap_index
        valid = (docs_ext[offset : offset + count] == docs_out) & (
            ext_pos[offset : offset + count] >= 0
        )
        term = taps[tap_index].astype(jnp.float32)[None, :] * extended[
            offset : offset + count
        ].astype(jnp.float32)
        running = running + jnp.where(valid[:, None], term, 0.0)
    return jax.nn.silu(running).astype(jnp.bfloat16)


def stretch_terms(x_rows, b_rows, c_rows, dt_rows, positions, doc_starts, dt_bias, decay_rate):
    count = positions.shape[0]
    heads = x_rows.shape[1] // MP
    groups = b_rows.shape[1] // MN
    per_group = heads // groups
    docs = doc_index(positions, doc_starts)
    prior_doc = doc_index(positions[:1] - 1, doc_starts)[0]
    delta = jax.nn.softplus(dt_rows.astype(jnp.float32) + dt_bias[None, :])
    log_decay = -delta * decay_rate[None, :]
    running = jnp.cumsum(log_decay, axis=0)
    running_heads = running.T
    order = jnp.arange(count, dtype=jnp.int32)
    causal = order[:, None] >= order[None, :]
    same_doc = docs[:, None] == docs[None, :]
    gaps = running_heads[:, :, None] - running_heads[:, None, :]
    segment = jnp.where((causal & same_doc)[None], jnp.exp(jnp.minimum(gaps, 0.0)), 0.0)
    inputs3 = x_rows.reshape(count, heads, MP)
    b_groups = b_rows.reshape(count, groups, MN)
    c_groups = c_rows.reshape(count, groups, MN)
    cross = jnp.einsum("tgn,sgn->gts", c_groups, b_groups, preferred_element_type=jnp.float32)
    cross_heads = jnp.repeat(cross, per_group, axis=0)
    mixing = (segment * cross_heads * delta.T[:, None, :]).astype(jnp.bfloat16)
    intra = jnp.einsum("hts,shp->thp", mixing, inputs3, preferred_element_type=jnp.float32)
    last_doc = docs[count - 1]
    to_end = (
        jnp.where((docs == last_doc)[:, None], jnp.exp(running[count - 1][None, :] - running), 0.0)
        * delta
    )
    weighted = (inputs3.astype(jnp.float32) * to_end[:, :, None]).astype(jnp.bfloat16)
    b_heads = jnp.repeat(b_groups, per_group, axis=1)
    local_state = jnp.einsum("shp,shn->hpn", weighted, b_heads, preferred_element_type=jnp.float32)
    carry_factor = jnp.where(prior_doc == last_doc, jnp.exp(running[count - 1]), 0.0)
    inflow = jnp.where((docs == prior_doc)[:, None], jnp.exp(running), 0.0)
    c_heads = jnp.repeat(c_groups, per_group, axis=1)
    return (intra, local_state, carry_factor, inflow, c_heads)


def stretch_finish(intra, incoming, inflow, c_heads, x_rows, skip_gain, norm_gain):
    count = x_rows.shape[0]
    heads = x_rows.shape[1] // MP
    incoming_bf = incoming.astype(jnp.bfloat16)
    entering = (
        jnp.einsum("thn,hpn->thp", c_heads, incoming_bf, preferred_element_type=jnp.float32)
        * inflow[:, :, None]
    )
    inputs3 = x_rows.reshape(count, heads, MP).astype(jnp.float32)
    mixed = intra + entering + skip_gain[None, :, None] * inputs3
    mean_square = jnp.mean(mixed * mixed, axis=-1, keepdims=True)
    normed = mixed * lax.rsqrt(mean_square + EPS_NORM) * norm_gain.reshape(heads, MP)[None]
    return normed.reshape(count, heads * MP).astype(jnp.bfloat16)


def combine_states(earlier, later):
    return (earlier[0] * later[0], later[0][:, None, None] * earlier[1] + later[1])


def local(
    queries,
    keys,
    values,
    mamba_x,
    mamba_b,
    mamba_c,
    mamba_dt,
    conv_x,
    conv_b,
    conv_c,
    dt_bias,
    decay_rate,
    skip_gain,
    norm_gain,
    windows,
    doc_lengths,
):
    served = (
        lax.all_to_all(queries, "tensor", split_axis=1, concat_axis=0, tiled=True),
        lax.all_to_all(keys, "tensor", split_axis=1, concat_axis=0, tiled=True),
        lax.all_to_all(values, "tensor", split_axis=1, concat_axis=0, tiled=True),
        lax.all_to_all(mamba_x, "tensor", split_axis=1, concat_axis=0, tiled=True),
        lax.all_to_all(mamba_b, "tensor", split_axis=1, concat_axis=0, tiled=True),
        lax.all_to_all(mamba_c, "tensor", split_axis=1, concat_axis=0, tiled=True),
        lax.all_to_all(mamba_dt, "tensor", split_axis=1, concat_axis=0, tiled=True),
    )
    query_rows, key_rows, value_rows, x_rows, b_rows, c_rows, dt_rows = served
    row_count = query_rows.shape[0]
    shard_start = lax.axis_index("seq") * row_count
    positions = shard_start + jnp.arange(row_count, dtype=jnp.int32)
    doc_starts = doc_table(doc_lengths)
    query_heads = query_rows.shape[1] // HEAD_SIZE
    shared_heads = key_rows.shape[1] // HEAD_SIZE
    group_width = query_heads // shared_heads
    window_per_head = lax.dynamic_slice_in_dim(
        windows, lax.axis_index("tensor") * query_heads, query_heads
    ).reshape(shared_heads, group_width)
    reach = jnp.max(window_per_head)
    grouped_heads = query_rows.reshape(row_count, shared_heads, group_width, HEAD_SIZE)
    initial = (
        jnp.full((shared_heads, group_width, row_count), NEG_LARGE, jnp.float32),
        jnp.zeros((shared_heads, group_width, row_count), jnp.float32),
        jnp.zeros((shared_heads, group_width, row_count, HEAD_SIZE), jnp.float32),
    )
    final = attend_piece(
        initial,
        (
            lax.all_gather(key_rows, "seq", axis=0, tiled=True),
            lax.all_gather(value_rows, "seq", axis=0, tiled=True),
        ),
        jnp.int32(0),
        grouped_heads,
        positions,
        doc_starts,
        window_per_head,
        reach,
    )
    final_max, totals, accum = final
    attention = (
        (accum / totals[..., None])
        .transpose(2, 0, 1, 3)
        .reshape(row_count, query_heads * HEAD_SIZE)
        .astype(jnp.bfloat16)
    )
    edge = row_count - (KC - 1)
    tails = shifted((x_rows[edge:], b_rows[edge:], c_rows[edge:]), "seq", 1)
    conv_x_out = causal_conv(
        jnp.concatenate([tails[0], x_rows], axis=0), conv_x, positions, doc_starts
    )
    conv_b_out = causal_conv(
        jnp.concatenate([tails[1], b_rows], axis=0), conv_b, positions, doc_starts
    )
    conv_c_out = causal_conv(
        jnp.concatenate([tails[2], c_rows], axis=0), conv_c, positions, doc_starts
    )
    intra, local_state, carry_factor, inflow, c_heads = stretch_terms(
        conv_x_out, conv_b_out, conv_c_out, dt_rows, positions, doc_starts, dt_bias, decay_rate
    )
    incoming = prefix(
        (carry_factor, local_state),
        "seq",
        combine_states,
        (jnp.ones_like(carry_factor), jnp.zeros_like(local_state)),
    )
    mamba_out = stretch_finish(
        intra, incoming[1], inflow, c_heads, conv_x_out, skip_gain, norm_gain
    )
    sums = lax.psum(
        (
            jnp.sum(attention.astype(jnp.float32), axis=0),
            jnp.sum(mamba_out.astype(jnp.float32), axis=0),
        ),
        "seq",
    )
    return (attention, mamba_out, sums[0], sums[1])


def solution(mesh):
    placed = (
        P(("seq", "tensor"), None),
        P(("seq", "tensor"), None),
        P(("seq", "tensor"), None),
        P(("seq", "tensor"), None),
        P(("seq", "tensor"), None),
        P(("seq", "tensor"), None),
        P(("seq", "tensor"), None),
        P(None, "tensor"),
        P(None, "tensor"),
        P(None, "tensor"),
        P("tensor"),
        P("tensor"),
        P("tensor"),
        P("tensor"),
        P(),
        P(),
    )
    return jax.shard_map(
        local,
        mesh=mesh,
        in_specs=placed,
        out_specs=(P("seq", "tensor"), P("seq", "tensor"), P("tensor"), P("tensor")),
        check_vma=False,
    )
```

profile of v0, /device:TPU:0, one launch (start us, length us, event | category | flops | bytes accessed | tf_op | source)
XLA Modules:
  0.0 185.0 jit_solution(2254786012537562026)
XLA Ops:
  7.2 0.8 all_to_all.107
  8.7 6.3 %all-to-all-start.4 = ((bf16[4,2,512]{2,1,0:T(2,128)(2,1)}), bf16[4,2,512]{2,1,0:T(2,128)(2,1)S(1)}, u32[]{:S(2)}, u32[]{:S(2)}) async-start(bf16[4,2,512]{2,1,0:T(2,128)(2,1)} %reshape.408), calls=%async_computation.4 | async-start | bytes 16384 | tf_op jit(solution)/shard_map/all_to_all | solution.py:186
  17.0 0.8 reduce-window.9
  17.8 1.3 fusion.30
  19.2 0.9 slice_convert_fusion.3
  20.1 0.8 slice_convert_fusion.7
  21.0 1.5 copy.168
  22.5 5.1 %all-to-all-start.6 = ((bf16[32,4,256]{2,0,1:T(8,128)(2,1)}), bf16[32,4,256]{2,0,1:T(8,128)(2,1)S(1)}, u32[]{:S(2)}, u32[]{:S(2)}) async-start(bf16[32,4,256]{2,0,1:T(8,128)(2,1)} %bitcast.129), calls=%async_computation.6 | async-start | bytes 131072 | tf_op jit(solution)/shard_map/all_to_all | solution.py:184
  28.1 1.9 %copy.166 = bf16[4,4,8,2048]{3,2,0,1:T(8,128)(2,1)} copy(bf16[4,4,8,2048]{3,2,1,0:T(8,128)(2,1)} %bitcast.155) | data formatting | bytes 1048576 | tf_op jit(solution)/shard_map/all_to_all | solution.py:183
  30.6 2.7 %all-to-all-done.6 = bf16[32,4,256]{2,0,1:T(8,128)(2,1)S(1)} async-done(((bf16[32,4,256]{2,0,1:T(8,128)(2,1)}), bf16[32,4,256]{2,0,1:T(8,128)(2,1)S(1)}, u32[]{:S(2)}, u32[]{:S(2)}) %all-to-all-start.6) | async-done | bytes 65568 | tf_op jit(solution)/shard_map/all_to_all | solution.py:184
  33.3 3.6 %all-to-all-start.3 = ((bf16[32,4,2048]{2,0,1:T(8,128)(2,1)}), bf16[32,4,2048]{2,0,1:T(8,128)(2,1)S(1)}, u32[]{:S(2)}, u32[]{:S(2)}) async-start(bf16[32,4,2048]{2,0,1:T(8,128)(2,1)} %bitcast.127), calls=%async_computation.3 | async-start | bytes 1048576 | tf_op jit(solution)/shard_map/all_to_all | solution.py:183
  39.4 1.3 collective-permute-start.2
  40.7 0.8 select_multiply_fusion
  41.5 8.2 %all-to-all-done.3 = bf16[32,4,2048]{2,0,1:T(8,128)(2,1)S(1)} async-done(((bf16[32,4,2048]{2,0,1:T(8,128)(2,1)}), bf16[32,4,2048]{2,0,1:T(8,128)(2,1)S(1)}, u32[]{:S(2)}, u32[]{:S(2)}) %all-to-all-start.3) | async-done | bytes 524320 | tf_op jit(solution)/shard_map/all_to_all | solution.py:183
  49.7 1.3 collective-permute-start
  51.8 1.0 multiply_convert_fusion.1
  53.3 1.2 convolution_convert_fusion
  55.2 3.3 %all-to-all-start.5 = ((bf16[32,4,256]{2,0,1:T(8,128)(2,1)}), bf16[32,4,256]{2,0,1:T(8,128)(2,1)S(1)}, u32[]{:S(2)}, u32[]{:S(2)}) async-start(bf16[32,4,256]{2,0,1:T(8,128)(2,1)} %bitcast.130), calls=%async_computation.5 | async-start | bytes 131072 | tf_op jit(solution)/shard_map/all_to_all | solution.py:185
  61.3 2.9 %all-to-all-done.5 = bf16[32,4,256]{2,0,1:T(8,128)(2,1)S(1)} async-done(((bf16[32,4,256]{2,0,1:T(8,128)(2,1)}), bf16[32,4,256]{2,0,1:T(8,128)(2,1)S(1)}, u32[]{:S(2)}, u32[]{:S(2)}) %all-to-all-start.5) | async-done | bytes 65568 | tf_op jit(solution)/shard_map/all_to_all | solution.py:185
  64.2 3.3 %all-to-all-start = ((bf16[32,4,256]{2,0,1:T(8,128)(2,1)}), bf16[32,4,256]{2,0,1:T(8,128)(2,1)S(1)}, u32[]{:S(2)}, u32[]{:S(2)}) async-start(bf16[32,4,256]{2,0,1:T(8,128)(2,1)} %bitcast.132), calls=%async_computation | async-start | bytes 131072 | tf_op jit(solution)/shard_map/all_to_all | solution.py:181
  67.5 1.3 fusion.31
  70.8 12.8 %all-gather.1 = bf16[8,1,32]{2,1,0:T(2,128)(2,1)S(1)} all-gather(bf16[1,1,32]{2,1,0:T(2,128)(2,1)S(1)} %get-tuple-element.210), channel_id=1, replica_groups=mesh['seq'=8,'tensor'=4] {'seq'}, dimensions={0}, use_global_device_ids=true | all-gather | bytes 576 | tf_op jit(solution)/shard_map/all_gather | solution.py:24
  85.0 2.2 %collective-permute-start.1 = (bf16[3,256]{1,0:T(4,128)(2,1)S(1)}, bf16[3,256]{1,0:T(4,128)(2,1)S(1)}, u32[]{:S(2)}, u32[]{:S(2)}) collective-permute-start(bf16[3,256]{1,0:T(4,128)(2,1)S(1)} %slice.170), channel_id=1, source_target_pairs={{0,4},{4,8},{8,12},{12,16},{16,20},{20,24},{24,28},{1,5},{5,9},{9,... | collective-permute-start | bytes 4616 | tf_op jit(solution)/shard_map/ppermute | solution.py:18
  87.2 5.1 %all-to-all-start.2 = ((bf16[32,4,256]{2,0,1:T(8,128)(2,1)}), bf16[32,4,256]{2,0,1:T(8,128)(2,1)S(1)}, u32[]{:S(2)}, u32[]{:S(2)}) async-start(bf16[32,4,256]{2,0,1:T(8,128)(2,1)} %bitcast.131), calls=%async_computation.2 | async-start | bytes 131072 | tf_op jit(solution)/shard_map/all_to_all | solution.py:182
  92.3 9.3 %all_gather.16 = bf16[1024,256]{1,0:T(8,128)(2,1)S(1)} all-gather(bf16[128,256]{1,0:T(8,128)(2,1)S(1)} %bitcast.162), channel_id=1, replica_groups=mesh['seq'=8,'tensor'=4] {'seq'}, dimensions={0}, use_global_device_ids=true | all-gather | bytes 589824 | tf_op jit(solution)/shard_map/all_gather | solution.py:209
  101.6 4.7 %all-to-all-start.1 = ((bf16[32,4,1024]{2,0,1:T(8,128)(2,1)}), bf16[32,4,1024]{2,0,1:T(8,128)(2,1)S(1)}, u32[]{:S(2)}, u32[]{:S(2)}) async-start(bf16[32,4,1024]{2,0,1:T(8,128)(2,1)} %bitcast.128), calls=%async_computation.1 | async-start | bytes 524288 | tf_op jit(solution)/shard_map/all_to_all | solution.py:180
  106.3 9.7 %all_gather.17 = bf16[1024,256]{1,0:T(8,128)(2,1)S(1)} all-gather(bf16[128,256]{1,0:T(8,128)(2,1)S(1)} %bitcast.163), channel_id=1, replica_groups=mesh['seq'=8,'tensor'=4] {'seq'}, dimensions={0}, use_global_device_ids=true | all-gather | bytes 589824 | tf_op jit(solution)/shard_map/all_gather | solution.py:210
  117.3 1.6 fusion.13
  118.9 13.4 %conditional.1 = (f32[2,4,128]{2,1,0:T(4,128)S(1)}, f32[2,4,128,128]{3,2,1,0:T(8,128)S(1)}) conditional(s32[]{:T(128)} %convert_element_type.180, () %tuple.30, (s32[128]{0:T(128)S(1)}, s32[1024]{0:T(1024)S(1)}, s32[1024]{0:T(1024)S(1)}, s32[3]{0:T(128)S(1)}, s32[1024]{0:T(1024)S(1)}, /*index=5*/s32[8]{0:T(128)}, bf16[1024,256]{1,0:T(8,128)(2,1)S(1)}, ...), branch_computations={%region_2.3_spmd, %region_3.8_spmd} | conditional | flops 557590656 | bytes 36501220 | solution.py:84
  119.1 0.9 compare_and_fusion.1
  120.9 0.9 reshape.367
  122.0 4.1 %fusion = (f32[2,4,128]{2,1,0:T(4,128)S(1)}, f32[2,1024,128,4]{2,1,3,0:T(8,128)}) fusion(s32[2,4]{1,0:T(2,128)S(1)} %lt.30, s32[128,1024]{0,1:T(8,128)S(1)} %broadcast_subtract_fusion, pred[128,1024]{0,1:T(8,128)(4,1)S(1)} %compare_and_fusion.1, bf16[128,2,4,128]{3,2,1,0:T(4,128)(2,1)S(1)} %reshape.368, bf16[1024,2,128,1]{2,1,0,3:T(2,128)(2,1)} %bitcast.156), kind=kOutput, calls=%fused_computation.3 | convolution fusion | flops 273677312 | bytes 5640224 | tf_op jit(solution)/shard_map/cond/branch_1_fun/tgqd,sgd->gqts/dot_general | solution.py:67
  126.3 4.3 %fusion.1 = f32[2,4,128,128]{3,2,1,0:T(8,128)S(1)} fusion(f32[2,1024,128,4]{2,1,3,0:T(8,128)} %get-tuple-element.206, f32[2,4,128]{2,1,0:T(4,128)S(1)} %broadcast_maximum_fusion, s32[2,4]{1,0:T(2,128)S(1)} %lt.30, s32[128,1024]{0,1:T(8,128)S(1)} %broadcast_subtract_fusion, pred[128,1024]{0,1:T(8,128)(4,1)S(1)} %compare_and_fusion.1, ...), kind=kOutput, calls=%fused_computation.4 | convolution fusion | flops 275775488 | bytes 5902368 | tf_op jit(solution)/shard_map/cond/branch_1_fun/gqts,sgd->gqtd/dot_general | solution.py:75
  130.6 1.6 fusion.3
  132.7 0.9 convert_element_type.183
  133.5 2.0 %convolution_bitcast_fusion.1 = f32[128,32,64]{0,2,1:T(8,128)S(1)} fusion(bf16[128,32,64]{0,2,1:T(8,128)(2,1)S(1)} %bitcast.140, bf16[32,128,128]{2,1,0:T(8,128)(2,1)} %fusion.13), kind=kOutput, calls=%fused_computation.32 | convolution fusion | flops 67108864 | bytes 2621440 | tf_op jit(solution)/shard_map/hts,shp->thp/dot_general | solution.py:127
  135.6 16.0 %while.14 = (s32[]{:T(128)}, f32[32,64,128]{2,1,0:T(8,128)S(1)}, s32[]{:T(128)}, bf16[8,32]{1,0:T(8,128)(2,1)}, bf16[8,32,64,128]{3,2,1,0:T(8,128)(2,1)}, /*index=5*/s32[]{:T(128)}, s32[]{:T(128)}) while((s32[]{:T(128)}, f32[32,64,128]{2,1,0:T(8,128)S(1)}, s32[]{:T(128)}, bf16[8,32]{1,0:T(8,128)(2,1)}, ...), condition=%wide.region_13.14_spmd.clone, body=%wide.region_12.13_spmd.clone.sunk | while | flops 1310756 | bytes 2621865 | solution.py:37
  136.3 1.3 fusion.41
  138.3 1.3 fusion.41
  140.3 1.3 fusion.41
  142.3 1.3 fusion.41
  144.3 1.3 fusion.41
  146.4 1.3 fusion.41
  148.4 1.3 fusion.41
  150.4 1.3 fusion.41
  151.9 0.9 multiply_reduce_fusion
  153.6 1.0 copy.131
  154.6 23.6 %all-reduce = (f32[1024]{0:T(1024)}, f32[2048]{0:T(1024)}) all-reduce(f32[1024]{0:T(1024)S(1)} %bitcast.175, f32[2048]{0:T(1024)S(1)} %reduce_sum.112), channel_id=1, replica_groups=mesh['seq'=8,'tensor'=4] {'seq'}, use_global_device_ids=true, to_apply=%region_16.17 | all-reduce | flops 3072 | bytes 24576 | tf_op jit(solution)/shard_map/psum | solution.py:249
  (99 shorter events, 19.6 us)
Async XLA Ops:
  8.7 13.8 %all-to-all-start.4 = ((bf16[4,2,512]{2,1,0:T(2,128)(2,1)}), bf16[4,2,512]{2,1,0:T(2,128)(2,1)S(1)}, u32[]{:S(2)}, u32[]{:S(2)}) async-start(bf16[4,2,512]{2,1,0:T(2,128)(2,1)} %reshape.408), calls=%async_computation.4 | async-start | bytes 16384 | tf_op jit(solution)/shard_map/all_to_all | solution.py:186
  22.5 10.8 %all-to-all-start.6 = ((bf16[32,4,256]{2,0,1:T(8,128)(2,1)}), bf16[32,4,256]{2,0,1:T(8,128)(2,1)S(1)}, u32[]{:S(2)}, u32[]{:S(2)}) async-start(bf16[32,4,256]{2,0,1:T(8,128)(2,1)} %bitcast.129), calls=%async_computation.6 | async-start | bytes 131072 | tf_op jit(solution)/shard_map/all_to_all | solution.py:184
  30.0 24.6 %copy-start.5 = (bf16[32,1024]{1,0:T(8,128)(2,1)S(1)}, bf16[32,1024]{1,0:T(8,128)(2,1)}, u32[]{:S(2)}) copy-start(bf16[32,1024]{1,0:T(8,128)(2,1)} %param.25) | copy-start | bytes 196612
  33.3 25.3 %copy-start.9 = (bf16[4,256]{1,0:T(4,128)(2,1)S(1)}, bf16[4,256]{1,0:T(4,128)(2,1)}, u32[]{:S(2)}) copy-start(bf16[4,256]{1,0:T(4,128)(2,1)} %param.29) | copy-start | bytes 6148
  33.3 25.3 %copy-start.8 = (f32[2048]{0:T(1024)S(1)}, f32[2048]{0:T(1024)}, u32[]{:S(2)}) copy-start(f32[2048]{0:T(1024)} %param.33) | copy-start | bytes 24580
  33.3 26.0 %copy-start.6 = (bf16[32,1024]{1,0:T(8,128)(2,1)S(1)}, bf16[32,1024]{1,0:T(8,128)(2,1)}, u32[]{:S(2)}) copy-start(bf16[32,1024]{1,0:T(8,128)(2,1)} %param.21) | copy-start | bytes 196612
  33.3 26.6 %copy-start.7 = (bf16[32,1024]{1,0:T(8,128)(2,1)S(1)}, bf16[32,1024]{1,0:T(8,128)(2,1)}, u32[]{:S(2)}) copy-start(bf16[32,1024]{1,0:T(8,128)(2,1)} %param.22) | copy-start | bytes 196612
  33.3 27.2 %copy-start.2 = (bf16[32,4096]{1,0:T(8,128)(2,1)S(1)}, bf16[32,4096]{1,0:T(8,128)(2,1)}, u32[]{:S(2)}) copy-start(bf16[32,4096]{1,0:T(8,128)(2,1)} %param.20) | copy-start | bytes 786436
  33.3 16.4 %all-to-all-start.3 = ((bf16[32,4,2048]{2,0,1:T(8,128)(2,1)}), bf16[32,4,2048]{2,0,1:T(8,128)(2,1)S(1)}, u32[]{:S(2)}, u32[]{:S(2)}) async-start(bf16[32,4,2048]{2,0,1:T(8,128)(2,1)} %bitcast.127), calls=%async_computation.3 | async-start | bytes 1048576 | tf_op jit(solution)/shard_map/all_to_all | solution.py:183
  36.9 30.6 %copy-start.11 = (s32[32]{0:T(128)S(1)}, s32[32]{0:T(128)}, u32[]{:S(2)}) copy-start(s32[32]{0:T(128)} %param.34) | copy-start | bytes 388
  37.0 98.6 %all-gather.4.cloned.1.call-start = ((), (), s32[]{:S(2)}) async-start(), calls=%async_computation.7 | async-start | bytes 4718592 | tf_op jit(solution)/shard_map/all_gather | solution.py:24
  39.4 11.6 %collective-permute-start.2 = (bf16[3,256]{1,0:T(4,128)(2,1)S(1)}, bf16[3,256]{1,0:T(4,128)(2,1)S(1)}, u32[]{:S(2)}, u32[]{:S(2)}) collective-permute-start(bf16[3,256]{1,0:T(4,128)(2,1)S(1)} %slice.175), channel_id=1, source_target_pairs={{0,4},{4,8},{8,12},{12,16},{16,20},{20,24},{24,28},{1,5},{5,9},{9,... | collective-permute-start | bytes 4616 | tf_op jit(solution)/shard_map/ppermute | solution.py:18
  49.7 2.1 %collective-permute-start = (bf16[3,2048]{1,0:T(4,128)(2,1)S(1)}, bf16[3,2048]{1,0:T(4,128)(2,1)S(1)}, u32[]{:S(2)}, u32[]{:S(2)}) collective-permute-start(bf16[3,2048]{1,0:T(4,128)(2,1)S(1)} %slice.165), channel_id=1, source_target_pairs={{0,4},{4,8},{8,12},{12,16},{16,20},{20,24},{24,28},{1,5},{5,9},{9,... | collective-permute-start | bytes 36872 | tf_op jit(solution)/shard_map/ppermute | solution.py:18
  55.2 9.0 %all-to-all-start.5 = ((bf16[32,4,256]{2,0,1:T(8,128)(2,1)}), bf16[32,4,256]{2,0,1:T(8,128)(2,1)S(1)}, u32[]{:S(2)}, u32[]{:S(2)}) async-start(bf16[32,4,256]{2,0,1:T(8,128)(2,1)} %bitcast.130), calls=%async_computation.5 | async-start | bytes 131072 | tf_op jit(solution)/shard_map/all_to_all | solution.py:185
  64.2 23.0 %all-to-all-start = ((bf16[32,4,256]{2,0,1:T(8,128)(2,1)}), bf16[32,4,256]{2,0,1:T(8,128)(2,1)S(1)}, u32[]{:S(2)}, u32[]{:S(2)}) async-start(bf16[32,4,256]{2,0,1:T(8,128)(2,1)} %bitcast.132), calls=%async_computation | async-start | bytes 131072 | tf_op jit(solution)/shard_map/all_to_all | solution.py:181
  85.0 31.1 %collective-permute-start.1 = (bf16[3,256]{1,0:T(4,128)(2,1)S(1)}, bf16[3,256]{1,0:T(4,128)(2,1)S(1)}, u32[]{:S(2)}, u32[]{:S(2)}) collective-permute-start(bf16[3,256]{1,0:T(4,128)(2,1)S(1)} %slice.170), channel_id=1, source_target_pairs={{0,4},{4,8},{8,12},{12,16},{16,20},{20,24},{24,28},{1,5},{5,9},{9,... | collective-permute-start | bytes 4616 | tf_op jit(solution)/shard_map/ppermute | solution.py:18
  87.2 14.4 %all-to-all-start.2 = ((bf16[32,4,256]{2,0,1:T(8,128)(2,1)}), bf16[32,4,256]{2,0,1:T(8,128)(2,1)S(1)}, u32[]{:S(2)}, u32[]{:S(2)}) async-start(bf16[32,4,256]{2,0,1:T(8,128)(2,1)} %bitcast.131), calls=%async_computation.2 | async-start | bytes 131072 | tf_op jit(solution)/shard_map/all_to_all | solution.py:182
  101.6 17.3 %all-to-all-start.1 = ((bf16[32,4,1024]{2,0,1:T(8,128)(2,1)}), bf16[32,4,1024]{2,0,1:T(8,128)(2,1)S(1)}, u32[]{:S(2)}, u32[]{:S(2)}) async-start(bf16[32,4,1024]{2,0,1:T(8,128)(2,1)} %bitcast.128), calls=%async_computation.1 | async-start | bytes 524288 | tf_op jit(solution)/shard_map/all_to_all | solution.py:180
  126.3 4.4 %copy-start = (f32[2,1024,128,4]{2,1,3,0:T(8,128)S(1)}, f32[2,1024,128,4]{2,1,3,0:T(8,128)}, u32[]{:S(2)}) copy-start(f32[2,1024,128,4]{2,1,3,0:T(8,128)} %get-tuple-element.206) | copy-start | bytes 12582916 | tf_op jit(solution)/shard_map/cond
  135.6 16.1 %copy-start.1 = (bf16[128,2,128]{2,0,1:T(8,128)(2,1)S(1)}, bf16[128,2,128]{2,0,1:T(8,128)(2,1)}, u32[]{:S(2)}) copy-start(bf16[128,2,128]{2,0,1:T(8,128)(2,1)} %copy.129) | copy-start | bytes 196612
  135.6 16.3 %copy-start.3 = (f32[128,32]{0,1:T(8,128)S(1)}, f32[128,32]{0,1:T(8,128)}, u32[]{:S(2)}) copy-start(f32[128,32]{0,1:T(8,128)} %copy.130) | copy-start | bytes 49156
  135.6 16.3 %copy-start.10 = (f32[32]{0:T(128)S(1)}, f32[32]{0:T(128)}, u32[]{:S(2)}) copy-start(f32[32]{0:T(128)} %param.32) | copy-start | bytes 388
  151.7 1.2 copy-start.4
Sparse Core Ops, SparseCore 0:
  54.7 38.6 all-gather.3
where the time goes:
time: 187 us; the launch traced here: 185 us
  blocking collectives  55.4 us (30%)
  starting transfers between devices  36.3 us (19%)
  other arithmetic  30.3 us (16%)
  between operations  19 us (10%)
  local copies, waits for them, and re-layouts  16.8 us (9%)
  waiting for transfers between devices  14.2 us (8%)
  matrix products  12.8 us (7%)
    psum x1, blocking collectives, local(): lax.psum((jnp.sum(attention.astype(jnp.float32), axis=0), jnp.sum(mamba_o...  23.6 us
    all_gather x1, blocking collectives, prefix(): lax.all_gather(part.astype(kind), axis)  12.8 us
    select_n x8, other arithmetic, turn(): return jax.tree.map(lambda a, b: jnp.where(reached, a, b), new, before)  10.4 us
    all_gather x1, blocking collectives, local(): lax.all_gather(value_rows, 'seq', axis=0, tiled=True)  9.74 us
    all_gather x1, blocking collectives, local(): lax.all_gather(key_rows, 'seq', axis=0, tiled=True)  9.29 us
    all_to_all x1, waiting for transfers between devices, local(): lax.all_to_all(mamba_x, 'tensor', split_axis=1, concat_axis=0, tiled=True)  8.17 us
    all_to_all x1, starting transfers between devices, local(): lax.all_to_all(mamba_dt, 'tensor', split_axis=1, concat_axis=0, tiled=True)  6.35 us
    convert_element_type x8, other arithmetic, turn(): part[k].astype(own.dtype)  5.54 us
  transfers between devices with their start and end apart: 11, of which 4 were waited for; matrix products, arithmetic and copies ran while one was open for 20% of the time, Pallas kernels for 0%

commit v1 on v0

--- a/solution.py
+++ b/solution.py
@@ -3,6 +3,7 @@
 import jax.numpy as jnp
 from jax import lax
 from jax.sharding import PartitionSpec as P
+from jax.lax import all_to_all, axis_size
 
 HEAD_SIZE = 128
 MP = 64
@@ -10,6 +11,12 @@
 KC = 4
 NEG_LARGE = -1e30
 EPS_NORM = 1e-05
+
+
+def pages_number(tile_in, axis_name):
+    local_part = jnp.stack(jnp.split(tile_in, axis_size(axis_name), axis=1), axis=0)
+    side_arr = all_to_all(local_part, axis_name=axis_name, split_axis=0, concat_axis=0)
+    return jnp.concatenate(side_arr, 0)
 
 
 def shifted(block, axis, distance):
@@ -180,7 +187,7 @@
         lax.all_to_all(queries, "tensor", split_axis=1, concat_axis=0, tiled=True),
         lax.all_to_all(keys, "tensor", split_axis=1, concat_axis=0, tiled=True),
         lax.all_to_all(values, "tensor", split_axis=1, concat_axis=0, tiled=True),
-        lax.all_to_all(mamba_x, "tensor", split_axis=1, concat_axis=0, tiled=True),
+        pages_number(mamba_x, "tensor"),
         lax.all_to_all(mamba_b, "tensor", split_axis=1, concat_axis=0, tiled=True),
         lax.all_to_all(mamba_c, "tensor", split_axis=1, concat_axis=0, tiled=True),
         lax.all_to_all(mamba_dt, "tensor", split_axis=1, concat_axis=0, tiled=True),

time: 187 us -> 195 us (1.043)
  blocking collectives: 55.4 us -> 60.1 us
  waiting for transfers between devices: 14.2 us -> 16.6 us
  other arithmetic: 30.3 us -> 32.4 us
    all_gather x1, blocking collectives: 12.8 us -> 17.5 us  [prefix(): lax.all_gather(part.astype(kind), axis)]
  transfers between devices with their start and end apart: 11 -> 11, of which waited for: 4 -> 4; matrix products, arithmetic and copies ran while one was open for 20% -> 19% of each run, Pallas kernels for 0% -> 0%
where the time goes in v1:
time: 195 us; the launch traced here: 194 us
  blocking collectives  60.1 us (31%)
  starting transfers between devices  36.2 us (19%)
  other arithmetic  32.4 us (17%)
  between operations  19 us (10%)
  waiting for transfers between devices  16.6 us (9%)
  local copies, waits for them, and re-layouts  16.2 us (8%)
  matrix products  12.8 us (7%)
    psum x1, blocking collectives, local(): lax.psum((jnp.sum(attention.astype(jnp.float32), axis=0), jnp.sum(mamba_o...  23.6 us
    all_gather x1, blocking collectives, prefix(): lax.all_gather(part.astype(kind), axis)  17.5 us
    select_n x8, other arithmetic, turn(): return jax.tree.map(lambda a, b: jnp.where(reached, a, b), new, before)  10.4 us
    all_gather x1, blocking collectives, local(): lax.all_gather(value_rows, 'seq', axis=0, tiled=True)  9.74 us
    all_gather x1, blocking collectives, local(): lax.all_gather(key_rows, 'seq', axis=0, tiled=True)  9.29 us
    all_to_all x1, waiting for transfers between devices, pages_number(): all_to_all(local_part, axis_name=axis_name, split_axis=0, concat_axis=0)  8.13 us
    all_to_all x1, starting transfers between devices, local(): lax.all_to_all(mamba_dt, 'tensor', split_axis=1, concat_axis=0, tiled=True)  6.35 us
    convert_element_type x8, other arithmetic, turn(): part[k].astype(own.dtype)  5.54 us
  transfers between devices with their start and end apart: 11, of which 4 were waited for; matrix products, arithmetic and copies ran while one was open for 19% of the time, Pallas kernels for 0%

profile of v1, /device:TPU:0, one launch (start us, length us, event | category | flops | bytes accessed | tf_op | source)
XLA Modules:
  0.0 193.6 jit_solution(13610859817464591192)
XLA Ops:
  8.7 6.3 %all-to-all-start.4 = ((bf16[4,2,512]{2,1,0:T(2,128)(2,1)}), bf16[4,2,512]{2,1,0:T(2,128)(2,1)S(1)}, u32[]{:S(2)}, u32[]{:S(2)}) async-start(bf16[4,2,512]{2,1,0:T(2,128)(2,1)} %reshape.409), calls=%async_computation.4 | async-start | bytes 16384 | tf_op jit(solution)/shard_map/all_to_all | solution.py:193
  16.9 0.8 reduce-window.9
  17.7 1.4 fusion.30
  19.2 1.1 slice_bitcast_fusion.3
  20.3 0.9 slice_convert_fusion.3
  21.2 0.8 slice_convert_fusion.7
  22.0 0.9 pad_maximum_fusion.1
  23.0 1.5 copy.172
  24.5 5.1 %all-to-all-start.6 = ((bf16[32,4,256]{2,0,1:T(8,128)(2,1)}), bf16[32,4,256]{2,0,1:T(8,128)(2,1)S(1)}, u32[]{:S(2)}, u32[]{:S(2)}) async-start(bf16[32,4,256]{2,0,1:T(8,128)(2,1)} %bitcast.131), calls=%async_computation.6 | async-start | bytes 131072 | tf_op jit(solution)/shard_map/all_to_all | solution.py:191
  30.8 4.5 %all-to-all-done.6 = bf16[32,4,256]{2,0,1:T(8,128)(2,1)S(1)} async-done(((bf16[32,4,256]{2,0,1:T(8,128)(2,1)}), bf16[32,4,256]{2,0,1:T(8,128)(2,1)S(1)}, u32[]{:S(2)}, u32[]{:S(2)}) %all-to-all-start.6) | async-done | bytes 65568 | tf_op jit(solution)/shard_map/all_to_all | solution.py:191
  35.3 3.5 %all-to-all-start.3 = ((bf16[4,32,2048]{2,1,0:T(8,128)(2,1)}), bf16[4,32,2048]{2,1,0:T(8,128)(2,1)S(1)}, u32[]{:S(2)}, u32[]{:S(2)}) async-start(bf16[4,32,2048]{2,1,0:T(8,128)(2,1)} %pad_maximum_fusion.1), calls=%async_computation.3 | async-start | bytes 1048576 | tf_op jit(solution)/shard_map/all_to_all | solution.py:18
  41.2 1.3 collective-permute-start.2
  43.4 8.1 %all-to-all-done.3 = bf16[4,32,2048]{2,1,0:T(8,128)(2,1)S(1)} async-done(((bf16[4,32,2048]{2,1,0:T(8,128)(2,1)}), bf16[4,32,2048]{2,1,0:T(8,128)(2,1)S(1)}, u32[]{:S(2)}, u32[]{:S(2)}) %all-to-all-start.3) | async-done | bytes 524320 | tf_op jit(solution)/shard_map/all_to_all | solution.py:18
  52.0 1.3 collective-permute-start
  53.8 1.1 collective-permute-done
  54.8 2.2 %multiply_convert_fusion.1 = bf16[128,2048]{0,1:T(8,128)(2,1)S(1)} fusion(bf16[128,2048]{0,1:T(8,128)(2,1)S(1)} %copy.121, bf16[3,2048]{0,1:T(8,128)(2,1)S(1)} %collective-permute-done, f32[2048]{0:T(1024)S(1)} %bitcast.173, f32[2048]{0:T(1024)S(1)} %bitcast.174, f32[2048]{0:T(1024)S(1)} %bitcast.172, f32[2048]{0:T(1024)S(1)} %bitcast.171, ...), kind=kLoop, calls=%fused_computation.44 | loop fusion | flops 7602176 | bytes 1094144 | tf_op jit(solution)/shard_map/convert_element_type | solution.py:109
  57.3 1.2 convolution_convert_fusion
  59.1 3.3 %all-to-all-start.5 = ((bf16[32,4,256]{2,0,1:T(8,128)(2,1)}), bf16[32,4,256]{2,0,1:T(8,128)(2,1)S(1)}, u32[]{:S(2)}, u32[]{:S(2)}) async-start(bf16[32,4,256]{2,0,1:T(8,128)(2,1)} %bitcast.132), calls=%async_computation.5 | async-start | bytes 131072 | tf_op jit(solution)/shard_map/all_to_all | solution.py:192
  65.2 2.9 %all-to-all-done.5 = bf16[32,4,256]{2,0,1:T(8,128)(2,1)S(1)} async-done(((bf16[32,4,256]{2,0,1:T(8,128)(2,1)}), bf16[32,4,256]{2,0,1:T(8,128)(2,1)S(1)}, u32[]{:S(2)}, u32[]{:S(2)}) %all-to-all-start.5) | async-done | bytes 65568 | tf_op jit(solution)/shard_map/all_to_all | solution.py:192
  68.1 3.3 %all-to-all-start = ((bf16[32,4,256]{2,0,1:T(8,128)(2,1)}), bf16[32,4,256]{2,0,1:T(8,128)(2,1)S(1)}, u32[]{:S(2)}, u32[]{:S(2)}) async-start(bf16[32,4,256]{2,0,1:T(8,128)(2,1)} %bitcast.134), calls=%async_computation | async-start | bytes 131072 | tf_op jit(solution)/shard_map/all_to_all | solution.py:188
  71.4 1.2 fusion.31
  74.6 17.5 %all-gather.1 = bf16[8,1,32]{2,1,0:T(2,128)(2,1)S(1)} all-gather(bf16[1,1,32]{2,1,0:T(2,128)(2,1)S(1)} %get-tuple-element.214), channel_id=1, replica_groups=mesh['seq'=8,'tensor'=4] {'seq'}, dimensions={0}, use_global_device_ids=true | all-gather | bytes 576 | tf_op jit(solution)/shard_map/all_gather | solution.py:31
  93.6 2.2 %collective-permute-start.1 = (bf16[3,256]{1,0:T(4,128)(2,1)S(1)}, bf16[3,256]{1,0:T(4,128)(2,1)S(1)}, u32[]{:S(2)}, u32[]{:S(2)}) collective-permute-start(bf16[3,256]{1,0:T(4,128)(2,1)S(1)} %slice.170), channel_id=1, source_target_pairs={{0,4},{4,8},{8,12},{12,16},{16,20},{20,24},{24,28},{1,5},{5,9},{9,... | collective-permute-start | bytes 4616 | tf_op jit(solution)/shard_map/ppermute | solution.py:25
  95.8 5.1 %all-to-all-start.2 = ((bf16[32,4,256]{2,0,1:T(8,128)(2,1)}), bf16[32,4,256]{2,0,1:T(8,128)(2,1)S(1)}, u32[]{:S(2)}, u32[]{:S(2)}) async-start(bf16[32,4,256]{2,0,1:T(8,128)(2,1)} %bitcast.133), calls=%async_computation.2 | async-start | bytes 131072 | tf_op jit(solution)/shard_map/all_to_all | solution.py:189
  100.9 9.3 %all_gather.16 = bf16[1024,256]{1,0:T(8,128)(2,1)S(1)} all-gather(bf16[128,256]{1,0:T(8,128)(2,1)S(1)} %bitcast.162), channel_id=1, replica_groups=mesh['seq'=8,'tensor'=4] {'seq'}, dimensions={0}, use_global_device_ids=true | all-gather | bytes 589824 | tf_op jit(solution)/shard_map/all_gather | solution.py:216
  110.2 4.7 %all-to-all-start.1 = ((bf16[32,4,1024]{2,0,1:T(8,128)(2,1)}), bf16[32,4,1024]{2,0,1:T(8,128)(2,1)S(1)}, u32[]{:S(2)}, u32[]{:S(2)}) async-start(bf16[32,4,1024]{2,0,1:T(8,128)(2,1)} %bitcast.130), calls=%async_computation.1 | async-start | bytes 524288 | tf_op jit(solution)/shard_map/all_to_all | solution.py:187
  114.9 9.7 %all_gather.17 = bf16[1024,256]{1,0:T(8,128)(2,1)S(1)} all-gather(bf16[128,256]{1,0:T(8,128)(2,1)S(1)} %bitcast.163), channel_id=1, replica_groups=mesh['seq'=8,'tensor'=4] {'seq'}, dimensions={0}, use_global_device_ids=true | all-gather | bytes 589824 | tf_op jit(solution)/shard_map/all_gather | solution.py:217
  125.9 1.6 fusion.13
  127.5 13.3 %conditional.1 = (f32[2,4,128]{2,1,0:T(4,128)S(1)}, f32[2,4,128,128]{3,2,1,0:T(8,128)S(1)}) conditional(s32[]{:T(128)} %convert_element_type.180, () %tuple.30, (s32[128]{0:T(128)S(1)}, s32[1024]{0:T(1024)S(1)}, s32[1024]{0:T(1024)S(1)}, s32[3]{0:T(128)S(1)}, s32[1024]{0:T(1024)S(1)}, /*index=5*/s32[8]{0:T(128)}, bf16[1024,256]{1,0:T(8,128)(2,1)S(1)}, ...), branch_computations={%region_2.3_spmd, %region_3.8_spmd} | conditional | flops 557590656 | bytes 36501220 | solution.py:91
  127.7 0.9 compare_and_fusion.1
  129.5 0.9 reshape.366
  130.6 4.1 %fusion = (f32[2,4,128]{2,1,0:T(4,128)S(1)}, f32[2,1024,128,4]{2,1,3,0:T(8,128)}) fusion(s32[2,4]{1,0:T(2,128)S(1)} %lt.30, s32[128,1024]{0,1:T(8,128)S(1)} %broadcast_subtract_fusion, pred[128,1024]{0,1:T(8,128)(4,1)S(1)} %compare_and_fusion.1, bf16[128,2,4,128]{3,2,1,0:T(4,128)(2,1)S(1)} %reshape.367, bf16[1024,2,128,1]{2,1,0,3:T(2,128)(2,1)} %bitcast.156), kind=kOutput, calls=%fused_computation.3 | convolution fusion | flops 273677312 | bytes 5640224 | tf_op jit(solution)/shard_map/cond/branch_1_fun/tgqd,sgd->gqts/dot_general | solution.py:74
  134.8 4.3 %fusion.1 = f32[2,4,128,128]{3,2,1,0:T(8,128)S(1)} fusion(f32[2,1024,128,4]{2,1,3,0:T(8,128)} %get-tuple-element.206, f32[2,4,128]{2,1,0:T(4,128)S(1)} %broadcast_maximum_fusion, s32[2,4]{1,0:T(2,128)S(1)} %lt.30, s32[128,1024]{0,1:T(8,128)S(1)} %broadcast_subtract_fusion, pred[128,1024]{0,1:T(8,128)(4,1)S(1)} %compare_and_fusion.1, ...), kind=kOutput, calls=%fused_computation.4 | convolution fusion | flops 275775488 | bytes 5902368 | tf_op jit(solution)/shard_map/cond/branch_1_fun/gqts,sgd->gqtd/dot_general | solution.py:82
  139.2 1.6 fusion.3
  141.2 0.9 convert_element_type.183
  142.1 2.0 %convolution_bitcast_fusion.1 = f32[128,32,64]{0,2,1:T(8,128)S(1)} fusion(bf16[128,32,64]{0,2,1:T(8,128)(2,1)S(1)} %bitcast.142, bf16[32,128,128]{2,1,0:T(8,128)(2,1)} %fusion.13), kind=kOutput, calls=%fused_computation.32 | convolution fusion | flops 67108864 | bytes 2621440 | tf_op jit(solution)/shard_map/hts,shp->thp/dot_general | solution.py:134
  144.2 16.0 %while.14 = (s32[]{:T(128)}, f32[32,64,128]{2,1,0:T(8,128)S(1)}, s32[]{:T(128)}, bf16[8,32]{1,0:T(8,128)(2,1)}, bf16[8,32,64,128]{3,2,1,0:T(8,128)(2,1)}, /*index=5*/s32[]{:T(128)}, s32[]{:T(128)}) while((s32[]{:T(128)}, f32[32,64,128]{2,1,0:T(8,128)S(1)}, s32[]{:T(128)}, bf16[8,32]{1,0:T(8,128)(2,1)}, ...), condition=%wide.region_13.14_spmd.clone, body=%wide.region_12.13_spmd.clone.sunk | while | flops 1310756 | bytes 2621865 | solution.py:44
  144.9 1.3 fusion.41
  146.9 1.3 fusion.41
  148.9 1.3 fusion.41
  150.9 1.3 fusion.41
  152.9 1.3 fusion.41
  154.9 1.3 fusion.41
  156.9 1.3 fusion.41
  158.9 1.3 fusion.41
  160.5 0.9 multiply_reduce_fusion
  162.1 1.0 copy.138
  163.1 23.6 %all-reduce = (f32[1024]{0:T(1024)}, f32[2048]{0:T(1024)}) all-reduce(f32[1024]{0:T(1024)S(1)} %bitcast.175, f32[2048]{0:T(1024)S(1)} %reduce_sum.112), channel_id=1, replica_groups=mesh['seq'=8,'tensor'=4] {'seq'}, use_global_device_ids=true, to_apply=%region_16.17 | all-reduce | flops 3072 | bytes 24576 | tf_op jit(solution)/shard_map/psum | solution.py:256
  (100 shorter events, 20.9 us)
Async XLA Ops:
  8.7 15.8 %all-to-all-start.4 = ((bf16[4,2,512]{2,1,0:T(2,128)(2,1)}), bf16[4,2,512]{2,1,0:T(2,128)(2,1)S(1)}, u32[]{:S(2)}, u32[]{:S(2)}) async-start(bf16[4,2,512]{2,1,0:T(2,128)(2,1)} %reshape.409), calls=%async_computation.4 | async-start | bytes 16384 | tf_op jit(solution)/shard_map/all_to_all | solution.py:193
  24.5 10.8 %all-to-all-start.6 = ((bf16[32,4,256]{2,0,1:T(8,128)(2,1)}), bf16[32,4,256]{2,0,1:T(8,128)(2,1)S(1)}, u32[]{:S(2)}, u32[]{:S(2)}) async-start(bf16[32,4,256]{2,0,1:T(8,128)(2,1)} %bitcast.131), calls=%async_computation.6 | async-start | bytes 131072 | tf_op jit(solution)/shard_map/all_to_all | solution.py:191
  35.3 16.2 %all-to-all-start.3 = ((bf16[4,32,2048]{2,1,0:T(8,128)(2,1)}), bf16[4,32,2048]{2,1,0:T(8,128)(2,1)S(1)}, u32[]{:S(2)}, u32[]{:S(2)}) async-start(bf16[4,32,2048]{2,1,0:T(8,128)(2,1)} %pad_maximum_fusion.1), calls=%async_computation.3 | async-start | bytes 1048576 | tf_op jit(solution)/shard_map/all_to_all | solution.py:18
  38.8 105.3 %all-gather.4.cloned.1.call-start = ((), (), s32[]{:S(2)}) async-start(), calls=%async_computation.7 | async-start | bytes 4718592 | tf_op jit(solution)/shard_map/all_gather | solution.py:31
  41.0 17.5 %copy-start.5 = (bf16[32,1024]{1,0:T(8,128)(2,1)S(1)}, bf16[32,1024]{1,0:T(8,128)(2,1)}, u32[]{:S(2)}) copy-start(bf16[32,1024]{1,0:T(8,128)(2,1)} %param.25) | copy-start | bytes 196612
  41.2 12.1 %collective-permute-start.2 = (bf16[3,256]{1,0:T(4,128)(2,1)S(1)}, bf16[3,256]{1,0:T(4,128)(2,1)S(1)}, u32[]{:S(2)}, u32[]{:S(2)}) collective-permute-start(bf16[3,256]{1,0:T(4,128)(2,1)S(1)} %slice.175), channel_id=1, source_target_pairs={{0,4},{4,8},{8,12},{12,16},{16,20},{20,24},{24,28},{1,5},{5,9},{9,... | collective-permute-start | bytes 4616 | tf_op jit(solution)/shard_map/ppermute | solution.py:25
  43.3 19.2 %copy-start.9 = (bf16[4,256]{1,0:T(4,128)(2,1)S(1)}, bf16[4,256]{1,0:T(4,128)(2,1)}, u32[]{:S(2)}) copy-start(bf16[4,256]{1,0:T(4,128)(2,1)} %param.29) | copy-start | bytes 6148
  43.3 19.2 %copy-start.8 = (f32[2048]{0:T(1024)S(1)}, f32[2048]{0:T(1024)}, u32[]{:S(2)}) copy-start(f32[2048]{0:T(1024)} %param.33) | copy-start | bytes 24580
  43.3 19.9 %copy-start.6 = (bf16[32,1024]{1,0:T(8,128)(2,1)S(1)}, bf16[32,1024]{1,0:T(8,128)(2,1)}, u32[]{:S(2)}) copy-start(bf16[32,1024]{1,0:T(8,128)(2,1)} %param.21) | copy-start | bytes 196612
  43.4 20.5 %copy-start.7 = (bf16[32,1024]{1,0:T(8,128)(2,1)S(1)}, bf16[32,1024]{1,0:T(8,128)(2,1)}, u32[]{:S(2)}) copy-start(bf16[32,1024]{1,0:T(8,128)(2,1)} %param.22) | copy-start | bytes 196612
  51.5 13.0 %copy-start.2 = (bf16[32,4096]{1,0:T(8,128)(2,1)S(1)}, bf16[32,4096]{1,0:T(8,128)(2,1)}, u32[]{:S(2)}) copy-start(bf16[32,4096]{1,0:T(8,128)(2,1)} %param.20) | copy-start | bytes 786436
  51.8 19.6 %copy-start.11 = (s32[32]{0:T(128)S(1)}, s32[32]{0:T(128)}, u32[]{:S(2)}) copy-start(s32[32]{0:T(128)} %param.34) | copy-start | bytes 388
  52.0 2.8 %collective-permute-start = (bf16[3,2048]{0,1:T(8,128)(2,1)S(1)}, bf16[3,2048]{0,1:T(8,128)(2,1)S(1)}, u32[]{:S(2)}, u32[]{:S(2)}) collective-permute-start(bf16[3,2048]{0,1:T(8,128)(2,1)S(1)} %slice.165), channel_id=1, source_target_pairs={{0,4},{4,8},{8,12},{12,16},{16,20},{20,24},{24,28},{1,5},{5,9},{9,... | collective-permute-start | bytes 36872 | tf_op jit(solution)/shard_map/ppermute | solution.py:25
  59.1 9.0 %all-to-all-start.5 = ((bf16[32,4,256]{2,0,1:T(8,128)(2,1)}), bf16[32,4,256]{2,0,1:T(8,128)(2,1)S(1)}, u32[]{:S(2)}, u32[]{:S(2)}) async-start(bf16[32,4,256]{2,0,1:T(8,128)(2,1)} %bitcast.132), calls=%async_computation.5 | async-start | bytes 131072 | tf_op jit(solution)/shard_map/all_to_all | solution.py:192
  68.1 27.7 %all-to-all-start = ((bf16[32,4,256]{2,0,1:T(8,128)(2,1)}), bf16[32,4,256]{2,0,1:T(8,128)(2,1)S(1)}, u32[]{:S(2)}, u32[]{:S(2)}) async-start(bf16[32,4,256]{2,0,1:T(8,128)(2,1)} %bitcast.134), calls=%async_computation | async-start | bytes 131072 | tf_op jit(solution)/shard_map/all_to_all | solution.py:188
  93.6 31.1 %collective-permute-start.1 = (bf16[3,256]{1,0:T(4,128)(2,1)S(1)}, bf16[3,256]{1,0:T(4,128)(2,1)S(1)}, u32[]{:S(2)}, u32[]{:S(2)}) collective-permute-start(bf16[3,256]{1,0:T(4,128)(2,1)S(1)} %slice.170), channel_id=1, source_target_pairs={{0,4},{4,8},{8,12},{12,16},{16,20},{20,24},{24,28},{1,5},{5,9},{9,... | collective-permute-start | bytes 4616 | tf_op jit(solution)/shard_map/ppermute | solution.py:25
  95.8 14.4 %all-to-all-start.2 = ((bf16[32,4,256]{2,0,1:T(8,128)(2,1)}), bf16[32,4,256]{2,0,1:T(8,128)(2,1)S(1)}, u32[]{:S(2)}, u32[]{:S(2)}) async-start(bf16[32,4,256]{2,0,1:T(8,128)(2,1)} %bitcast.133), calls=%async_computation.2 | async-start | bytes 131072 | tf_op jit(solution)/shard_map/all_to_all | solution.py:189
  110.2 17.3 %all-to-all-start.1 = ((bf16[32,4,1024]{2,0,1:T(8,128)(2,1)}), bf16[32,4,1024]{2,0,1:T(8,128)(2,1)S(1)}, u32[]{:S(2)}, u32[]{:S(2)}) async-start(bf16[32,4,1024]{2,0,1:T(8,128)(2,1)} %bitcast.130), calls=%async_computation.1 | async-start | bytes 524288 | tf_op jit(solution)/shard_map/all_to_all | solution.py:187
  134.8 4.4 %copy-start = (f32[2,1024,128,4]{2,1,3,0:T(8,128)S(1)}, f32[2,1024,128,4]{2,1,3,0:T(8,128)}, u32[]{:S(2)}) copy-start(f32[2,1024,128,4]{2,1,3,0:T(8,128)} %get-tuple-element.206) | copy-start | bytes 12582916 | tf_op jit(solution)/shard_map/cond
  144.1 16.1 %copy-start.1 = (bf16[128,2,128]{2,0,1:T(8,128)(2,1)S(1)}, bf16[128,2,128]{2,0,1:T(8,128)(2,1)}, u32[]{:S(2)}) copy-start(bf16[128,2,128]{2,0,1:T(8,128)(2,1)} %copy.136) | copy-start | bytes 196612
  144.2 16.3 %copy-start.3 = (f32[128,32]{0,1:T(8,128)S(1)}, f32[128,32]{0,1:T(8,128)}, u32[]{:S(2)}) copy-start(f32[128,32]{0,1:T(8,128)} %copy.137) | copy-start | bytes 49156
  144.2 16.3 %copy-start.10 = (f32[32]{0:T(128)S(1)}, f32[32]{0:T(128)}, u32[]{:S(2)}) copy-start(f32[32]{0:T(128)} %param.32) | copy-start | bytes 388
  160.2 1.2 copy-start.4
Sparse Core Ops, SparseCore 0:
  58.6 43.3 all-gather.3
